TPU v7x, 128 devices: a whole 4x4x4 slice. The times are simulated.
128 devices in a mesh: row: 16 (over y, x), col: 8 (over z, core).
Axes of the slice: x: 4, y: 4, z: 4, core: 2. Of those that a mesh axis runs over, the one named last changes fastest.
Arguments:
- ancestor_inverse: float32 [20480, 20480], P('row', 'col'), may hold values from -0.3125 to 0.3125
- panel_parent: float32 [20480, 512], P('row'), may hold values from -0.5 to 0.5
- panel_child: float32 [20480, 512], P('row'), may hold values from -0.5 to 0.5
- coupling: float32 [512, 512], replicated, may hold values from -0.125 to 0.125
- diag_parent: float32 [512, 512], replicated, may hold values from -3 to 3
- diag_child: float32 [512, 512], replicated, may hold values from -3 to 3
- structure: int32 [2, 160], replicated, may hold values from 0 to 1, as said below
Outputs:
- parent_rows: float32 [20480, 512], P(('row', 'col'))
- parent_diag: float32 [512, 512], P(('row', 'col'))
- child_top: float32 [512, 512], P(('row', 'col'))
- child_rows: float32 [20480, 512], P(('row', 'col'))
- child_diag: float32 [512, 512], P(('row', 'col'))
Inputs may be any that keep to these rules, and one draw needn't show every extreme that they name: `structure`: every entry is a flag of one block of 128 ancestor rows; a block flagged in row 1 is flagged in row 0, and the last block is flagged in both rows.
All inputs are finite; a program needn't handle non-finite values.
Results may differ from a plain program's by a relative error of at most 0.00007.
Values sent between devices are 32-bit elements; how exact they have to be, the bound alone decides.
No kernel may reach another device: no remote copies, remote signals or barrier semaphores. Data moves between devices by JAX's collectives and lax.ppermute only.
A program may use at most 128 MiB of HBM per device.

v0:
```python
import jax
import jax.numpy as jnp
from jax import lax
from jax.experimental import pallas as pl
from jax.experimental.pallas import tpu as pltpu
from jax.sharding import PartitionSpec as P


BLK = 128
SUB = 8
SIDE = 4
CORES = 2
RING = SIDE * SIDE
TILE_BLOCKS = 10
COL_BLOCKS = 20
GROUP = 160
W = 512
AXES = ("row", "col")
SLOTS = 32
CHUNKS = ((0, 6), (6, 10))


def device(y, x, z, core):
    return ((y % SIDE) * SIDE + x % SIDE) * SIDE * CORES + (z % SIDE) * CORES + core


def pairs(target):
    return [
        (device(y, x, z, core), device(*target(y, x, z, core)))
        for y in range(SIDE)
        for x in range(SIDE)
        for z in range(SIDE)
        for core in range(CORES)
    ]


def stepped(axis, by):
    def target(y, x, z, core):
        along = axis[core]
        return y + by * (along == "y"), x + by * (along == "x"), z + by * (along == "z"), core

    return pairs(target)


PARTNER = pairs(lambda y, x, z, core: (y, x, z, 1 - core))


def spread_target(y, x, z, core, flip):
    turn = 2 * core + (x + flip) % 2
    return (y + turn) % SIDE, (x + z + turn) % SIDE, y, x // 2


SPREAD = [
    pairs(lambda y, x, z, core, flip=flip: spread_target(y, x, z, core, flip)) for flip in range(2)
]


def shift(value, axis, by):
    return lax.ppermute(value, AXES, stepped(axis, by))


def product(left, right):
    return jnp.dot(left, right, precision=lax.Precision.HIGH, preferred_element_type=jnp.float32)


def product_t(left, right):
    return lax.dot_general(
        left, right, (((0,), (0,)), ((), ())), precision=lax.Precision.HIGH,
        preferred_element_type=jnp.float32,
    )


def compact_body(turn, structure, first, second, share):
    col = lax.axis_index("col")
    near = (lax.axis_index("row") // SIDE + SIDE - col // CORES) % 2
    slot = -SLOTS * turn[0]
    for which in range(2):

        def step(block, slot):
            flag = structure[which, col * COL_BLOCKS + block]
            part = block // TILE_BLOCKS
            own = block - part * TILE_BLOCKS

            @pl.when((flag == 1) & (slot >= 0) & (slot < SLOTS))
            def _():
                share[slot] = jnp.where(part == near, first[which, own], second[which, own])

            return slot + flag

        slot = lax.fori_loop(0, COL_BLOCKS, step, slot)


def compact(turn, structure, first, second):
    smem = pl.BlockSpec(memory_space=pltpu.SMEM)
    vmem = pl.BlockSpec(memory_space=pltpu.VMEM)
    return pl.pallas_call(
        compact_body,
        in_specs=[smem, smem, vmem, vmem],
        out_specs=vmem,
        out_shape=jax.ShapeDtypeStruct((SLOTS, SUB, W), jnp.float32),
        name="compact",
    )(turn, structure, first, second)


def gather_near(own, axis):
    return shift(own, axis, 1), shift(own, axis, -1)


def gather_far(before, after, axis):
    half = before.shape[0] // 2
    return shift(before[:half], axis, 1), shift(after[half:], axis, -1)


def gather_line(share, axis):
    before, after = gather_near(share, axis)
    far_low, far_high = gather_far(before, after, axis)
    return share, after, jnp.concatenate([far_low, far_high]), before


def split(value):
    high = value.astype(jnp.bfloat16)
    low = (value - high.astype(jnp.float32)).astype(jnp.bfloat16)
    return high, low


def narrow_body(value, parts):
    for block in range(COL_BLOCKS):
        high, low = split(value[:, block * BLK : (block + 1) * BLK])
        parts[block, :, :BLK] = high
        parts[block, :, BLK:] = low


def narrow(inverse):
    rows, cols = inverse.shape
    return pl.pallas_call(
        narrow_body,
        grid=(TILE_BLOCKS,),
        in_specs=[pl.BlockSpec((BLK, cols), lambda at: (at, 0))],
        out_specs=pl.BlockSpec((COL_BLOCKS, BLK, 2 * BLK), lambda at: (0, at, 0)),
        out_shape=jax.ShapeDtypeStruct((COL_BLOCKS, rows, 2 * BLK), jnp.bfloat16),
        cost_estimate=pl.CostEstimate(flops=0, transcendentals=0, bytes_accessed=2 * inverse.size * 4),
        name="narrow",
    )(inverse)


def blank(*shapes):
    hbm = pl.BlockSpec(memory_space=pl.ANY)
    return pl.pallas_call(
        lambda *refs: None,
        out_specs=[hbm] * len(shapes),
        out_shape=[jax.ShapeDtypeStruct(shape, jnp.float32) for shape in shapes],
        name="blank",
    )()


def tile_body(turn, structure, parts, own, before, after, far_low, far_high, whole_old, *refs):
    whole, mine, theirs = refs[2:5]
    blocks, rows, left, panel, right, acc, panel_sem, tile_sems, out_sem = refs[5:]
    row = lax.axis_index("row")
    col = lax.axis_index("col")
    y, x, z, core = row // SIDE, row % SIDE, col // CORES, col % CORES

    pieces = [(own, 0, i, i) for i in range(SIDE)]
    pieces += [(after, 1, i, i) for i in range(SIDE)]
    pieces += [(before, 3, i, i) for i in range(SIDE)]
    pieces += [(far_low, 2, i, i) for i in range(2)]
    pieces += [(far_high, 2, i, i + 2) for i in range(2)]
    copies = []
    for ref, outer, at, inner in pieces:
        sub_y = (y + jnp.where(core == 0, outer, inner)) % SIDE
        sub_x = (x + jnp.where(core == 0, inner, outer)) % SIDE
        copies.append(
            pltpu.make_async_copy(
                ref.at[at],
                panel.at[pl.ds(0, SLOTS), sub_y * SIDE + sub_x],
                panel_sem.at[len(copies)],
            )
        )
    for copy in copies:
        copy.start()

    def scan_columns(which, count):
        def step(block, slot):
            flag = structure[which, col * COL_BLOCKS + block]

            @pl.when(flag == 1)
            def _():
                blocks[slot] = block

            return slot + flag

        return lax.fori_loop(0, COL_BLOCKS, step, count)

    def scan_rows(which):
        def step(block, slot):
            flag = structure[which, row * TILE_BLOCKS + block]

            @pl.when(flag == 1)
            def _():
                rows[which, slot] = block

            return slot + flag

        used = lax.fori_loop(0, TILE_BLOCKS, step, 0)

        def pad(at, _):
            rows[which, at] = TILE_BLOCKS
            return 0

        lax.fori_loop(used, TILE_BLOCKS, pad, 0)
        return used

    parents = scan_columns(0, 0)
    both = scan_columns(1, parents)
    parent_lines, child_lines = scan_rows(0), scan_rows(1)
    first = SLOTS * turn[0]
    last = first + SLOTS
    parent_begin, parent_end = jnp.minimum(first, parents), jnp.minimum(last, parents)
    child_begin = jnp.clip(first, parents, both)
    child_end = jnp.clip(last, parents, both)
    parent_steps = (parent_end - parent_begin + 1) // 2
    steps = parent_steps + (child_end - child_begin + 1) // 2

    def slots_of(step):
        is_child = step >= parent_steps
        slot = jnp.where(is_child, child_begin + 2 * (step - parent_steps), parent_begin + 2 * step)
        return slot, jnp.where(is_child, child_end, parent_end)

    def tile_copies(step):
        slot, end = slots_of(step)
        buffer = step % 2
        copies = []
        for at in range(2):
            block = blocks[jnp.minimum(slot + at, end - 1)]
            copies.append(
                pltpu.make_async_copy(
                    parts.at[block],
                    left.at[buffer, :, :, pl.ds(2 * at * BLK, 2 * BLK)],
                    tile_sems.at[buffer, at],
                )
            )
        return copies

    for ahead in range(2):

        @pl.when(ahead < steps)
        def _():
            for copy in tile_copies(ahead):
                copy.start()

    @pl.when(turn[0] == 0)
    def _():
        acc[...] = jnp.zeros_like(acc)

    @pl.when(turn[0] > 0)
    def _():
        old = pltpu.make_async_copy(whole_old, acc.at[:, pl.ds(0, TILE_BLOCKS)], out_sem.at[0])
        old.start()
        old.wait()

    panel[SLOTS] = jnp.zeros((BLK // SUB, SUB, W), jnp.float32)
    for copy in copies:
        copy.wait()

    def contract(which, lines, step):
        for copy in tile_copies(step):
            copy.wait()
        buffer = step % 2
        slot, end = slots_of(step)
        for at in range(2):
            here = jnp.where(slot + at < end, slot + at - first, SLOTS)
            high, low = split(panel[here].reshape(BLK, W))
            right[pl.ds(2 * at * BLK, BLK)] = high
            right[pl.ds((2 * at + 1) * BLK, BLK)] = high
            right[pl.ds((4 + at) * BLK, BLK)] = low

        for begin, stop in CHUNKS:

            @pl.when(lines > begin)
            def _():
                picked = [rows[which, at] for at in range(begin, stop)]
                value = jnp.concatenate(
                    [left[buffer, jnp.minimum(at, TILE_BLOCKS - 1)] for at in picked], axis=0
                )
                value = jnp.concatenate(
                    [value, value[:, :BLK], value[:, 2 * BLK : 3 * BLK]], axis=1
                )
                part = jnp.dot(value, right[...], preferred_element_type=jnp.float32)
                for index, at in enumerate(picked):
                    acc[which, at] += part[index * BLK : (index + 1) * BLK]

        @pl.when(step + 2 < steps)
        def _():
            for copy in tile_copies(step + 2):
                copy.start()

    flat = acc.reshape(2, (TILE_BLOCKS + 1) * BLK, W)
    out_copies = []
    for which in range(2):
        made = [(acc.at[which, pl.ds(0, TILE_BLOCKS)], whole.at[which])]
        for at in range(SIDE):
            level = (z + at) % SIDE
            for ref, side in ((mine, core), (theirs, 1 - core)):
                start = pl.multiple_of((level * CORES + side) * GROUP, 32)
                made.append((flat.at[which, pl.ds(start, GROUP)], ref.at[at, :, pl.ds(which * W, W)]))
        out_copies.append(
            [
                pltpu.make_async_copy(source, to, out_sem.at[len(made) * which + at])
                for at, (source, to) in enumerate(made)
            ]
        )

    def parent_step(step, _):
        contract(0, parent_lines, step)
        return 0

    def child_step(step, _):
        contract(1, child_lines, step)
        return 0

    lax.fori_loop(0, parent_steps, parent_step, 0)
    for copy in out_copies[0]:
        copy.start()
    lax.fori_loop(parent_steps, steps, child_step, 0)
    for copy in out_copies[1]:
        copy.start()
    for copy in out_copies[0] + out_copies[1]:
        copy.wait()


def tile_products(turn, structure, parts, lines, old):
    hbm = pl.BlockSpec(memory_space=pl.ANY)
    smem = pl.BlockSpec(memory_space=pltpu.SMEM)
    return pl.pallas_call(
        tile_body,
        in_specs=[smem, smem] + [hbm] * 9,
        out_specs=[hbm] * 3,
        out_shape=[jax.ShapeDtypeStruct(array.shape, array.dtype) for array in old],
        input_output_aliases={8: 0, 9: 1, 10: 2},
        scratch_shapes=[
            pltpu.SMEM((2 * COL_BLOCKS,), jnp.int32),
            pltpu.SMEM((2, TILE_BLOCKS), jnp.int32),
            pltpu.VMEM((2, TILE_BLOCKS, BLK, 4 * BLK), jnp.bfloat16),
            pltpu.VMEM((SLOTS + 1, BLK // SUB, SUB, W), jnp.float32),
            pltpu.VMEM((6 * BLK, W), jnp.bfloat16),
            pltpu.VMEM((2, TILE_BLOCKS + 1, BLK, W), jnp.float32),
            pltpu.SemaphoreType.DMA((16,)),
            pltpu.SemaphoreType.DMA((2, 2)),
            pltpu.SemaphoreType.DMA((18,)),
        ],
        name="tile_products",
    )(
        turn,
        structure,
        parts.reshape(COL_BLOCKS, TILE_BLOCKS, BLK, 2 * BLK),
        *lines,
        *old,
    )


def ring_sum(piece, axis):
    got = []
    for at in (1, 2, 3):
        got.append(shift(piece(at), axis, at))
    return piece(0) + got[0] + got[1] + got[2]


def final_sums(terms, chunks, up, down, y, x, z, core):
    half = W // CORES

    def columns(side):
        return jnp.concatenate(
            [lax.dynamic_slice_in_dim(term, side * half, half, 1) for term in terms], axis=1
        )

    def take(array, at, dim):
        return lax.dynamic_index_in_dim(array, at % SIDE, dim, keepdims=False)

    cut = chunks.shape[1] // 2
    got = lax.ppermute(columns(1 - core), AXES, PARTNER)
    value = columns(core) + got
    cube = value.reshape(SIDE, SIDE, SIDE, SUB, len(terms) * half)
    above = jnp.concatenate([chunks[1, :cut] + up, chunks[1, cut:]])
    below = jnp.concatenate([chunks[3, :cut], chunks[3, cut:] + down])
    above = shift(above, "zz", 1)
    below = shift(below, "zz", -1)
    flat = ring_sum(
        lambda at: jnp.where(core == 0, take(cube, y + at, 0), take(cube, x + at, 1)), "yx"
    )
    line = ring_sum(lambda at: take(flat, jnp.where(core == 0, x, y) + at, 0), "xy")
    value = ring_sum(lambda at: take(line, z + at, 0), "zz")
    value, above, below = lax.optimization_barrier((value, above, below))
    rows = chunks[0] + above + below
    low, high = value[: SUB // 2], value[SUB // 2 :]
    kept = jnp.where(core == 0, low, high)
    got = lax.ppermute(jnp.where(core == 0, high, low), AXES, PARTNER)
    left, right = jnp.where(core == 0, kept, got), jnp.where(core == 0, got, kept)
    sums = [
        jnp.concatenate([part[:, at * half : (at + 1) * half] for part in (left, right)], axis=1)
        for at in range(len(terms))
    ]
    return rows, sums


def invert(
    ancestor_inverse, panel_parent, panel_child, coupling, diag_parent, diag_child, structure
):
    row = lax.axis_index("row")
    col = lax.axis_index("col")
    y, x, z, core = row // SIDE, row % SIDE, col // CORES, col % CORES
    tile_rows = panel_parent.shape[0]
    group_rows = tile_rows // (SIDE * CORES)
    own_count = W // (RING * SIDE * CORES)
    own_start = (row * SIDE * CORES + col) * own_count

    panels = jnp.stack([panel_parent, panel_child]).reshape(2, TILE_BLOCKS, BLK // SUB, SUB, W)

    def slices(flip):
        to_y, to_x, _, _ = spread_target(y, x, z, core, flip)
        return lax.dynamic_index_in_dim(panels, to_y * SIDE + to_x, 2, keepdims=False)

    first = lax.ppermute(slices(0), AXES, SPREAD[0])
    second = lax.ppermute(slices(1), AXES, SPREAD[1])
    counts = structure.reshape(2, SIDE * CORES, COL_BLOCKS).sum(axis=(0, 2))
    turns = (jnp.max(counts) + SLOTS - 1) // SLOTS

    def one_turn(at, old):
        turn = jnp.reshape(at, (1,))
        share = compact(turn, structure, first, second)
        line = jnp.stack(gather_line(share, "xy"))
        near = gather_near(line, "yx")
        near, parts = lax.optimization_barrier((near, narrow(ancestor_inverse)))
        lines = (line, *near, *gather_far(*near, "yx"))
        return tuple(tile_products(turn, structure, parts, lines, old))

    start = tuple(
        blank((2, TILE_BLOCKS, BLK, W), (SIDE, GROUP, 2 * W), (SIDE, GROUP, 2 * W))
    )
    whole, mine, theirs = lax.fori_loop(0, turns, one_turn, start)
    parent_whole = whole[0].reshape(tile_rows, W)
    child_whole = whole[1].reshape(tile_rows, W)

    flags = lax.dynamic_slice_in_dim(structure[1], row * TILE_BLOCKS, TILE_BLOCKS)
    block_rows = jnp.arange(tile_rows, dtype=jnp.int32)[:, None] // BLK
    hits = (block_rows == jnp.arange(TILE_BLOCKS, dtype=jnp.int32)[None, :]) & (flags[None, :] == 1)
    mask_child = jnp.any(hits, axis=1)[:, None]
    child = jnp.where(mask_child, panel_child, 0)
    mask_group = lax.dynamic_slice_in_dim(mask_child, col * group_rows, group_rows, 0)

    def own_rows(values):
        return lax.dynamic_slice_in_dim(values, own_start, own_count, 0)

    base_top = product(diag_parent, coupling)
    coupling_cols = lax.dynamic_slice_in_dim(coupling, own_start, own_count, 1)
    base_child = own_rows(diag_child) + product_t(coupling_cols, base_top)

    chunks = mine + lax.ppermute(theirs, AXES, PARTNER)
    cut = GROUP // 2
    up = shift(chunks[2, :cut], "zz", 1)
    down = shift(chunks[2, cut:], "zz", -1)
    parent_term = product_t(panel_parent, parent_whole)
    cross = product_t(parent_whole, child)
    top_term = product(parent_term, coupling) - cross
    child_term = (
        product_t(coupling, top_term) - product_t(cross, coupling) + product_t(panel_child, child_whole)
    )
    rows, (parent_sum, top_sum, child_sum) = final_sums(
        [parent_term, top_term, child_term], chunks, up, down, y, x, z, core
    )
    parent_rows = -rows[:, :W]
    child_rows = -(rows[:, W:] + jnp.where(mask_group, product(parent_rows, coupling), 0))
    parent_diag = own_rows(diag_parent) + parent_sum
    child_top = -(own_rows(base_top) + top_sum)
    child_diag = base_child + child_sum
    return parent_rows, parent_diag, child_top, child_rows, child_diag


def solution(mesh):
    return jax.shard_map(
        invert,
        mesh=mesh,
        in_specs=(P("row", "col"), P("row", None), P("row", None), P(), P(), P(), P()),
        out_specs=(P(AXES, None),) * 5,
        check_vma=False,
    )
```

profile of v0, /device:TPU:1, one launch (start us, length us, event | category | flops | bytes accessed | tf_op | source)
XLA Modules:
  0.0 197.3 jit_solution(13325912251948615875)
XLA Ops:
  2.1 8.7 %collective-permute-start.8 = (f32[2,10,8,512]{3,2,1,0:T(8,128)S(1)}, f32[2,10,8,512]{3,2,1,0:T(8,128)S(1)}, u32[]{:S(2)}, u32[]{:S(2)}) collective-permute-start(f32[2,10,8,512]{3,2,1,0:T(8,128)S(1)} %get-tuple-element.152), channel_id=1, source_target_pairs={{0,0},{1,80},{2,8},{3,88},{4,16},{5,64},{6,24},{7,72},{8,48},{9,96... | collective-permute-start | bytes 983048 | tf_op jit(solution)/shard_map/ppermute | solution.py:422
  10.8 4.5 %collective-permute-start.9 = (f32[2,10,8,512]{3,2,1,0:T(8,128)S(1)}, f32[2,10,8,512]{3,2,1,0:T(8,128)}, u32[]{:S(2)}, u32[]{:S(2)}) collective-permute-start(f32[2,10,8,512]{3,2,1,0:T(8,128)S(1)} %get-tuple-element.151), channel_id=1, source_target_pairs={{0,40},{1,120},{2,48},{3,96},{4,56},{5,104},{6,32},{7,112},{8,8},{... | collective-permute-start | bytes 983048 | tf_op jit(solution)/shard_map/ppermute | solution.py:423
  16.9 13.2 %narrow.3 = bf16[20,1280,256]{2,1,0:T(8,128)(2,1)} custom-call(f32[1280,2560]{1,0:T(8,128)} %value), custom_call_target="tpu_custom_call" | custom-call | bytes 26214400 | tf_op jit(solution)/shard_map/while/body/narrow/pallas_call | solution.py:135
  30.3 77.2 %while.16 = (s32[]{:T(128)}, f32[2,10,128,512]{3,2,1,0:T(8,128)}, f32[4,160,1024]{2,1,0:T(8,128)}, f32[4,160,1024]{2,1,0:T(8,128)}, s32[]{:T(128)}, /*index=5*/s...) while((s32[]{:T(128)}, f32[2,10,128,512]{3,2,1,0:T(8,128)}, ...), condition=%wide.region_4.5_spmd, body=%wide.region_3.4_spmd.sunk | while | flops 1703938 | bytes 67109376 | solution.py:439
  30.3 2.6 %compact.3 = f32[32,8,512]{2,1,0:T(8,128)} custom-call(s32[1]{0:T(128)} %bitcast.123.turn, s32[2,160]{1,0:T(2,128)S(1)} %get-tuple-element.277.structure, f32[2,10,8,512]{3,2,1,0:T(8,128)S(1)} %get-tuple-element.278.first, f32[2,10,8,512]{3,2,1,0:T(8,128)} %get-tuple-element.279.second), custom_call_target="tpu_custom_call" | custom-call | tf_op jit(solution)/shard_map/while/body/compact/pallas_call | solution.py:96
  34.5 6.9 %collective-permute-done.1 = f32[32,8,512]{2,1,0:T(8,128)S(1)} collective-permute-done((f32[32,8,512]{2,1,0:T(8,128)}, f32[32,8,512]{2,1,0:T(8,128)S(1)}, u32[]{:S(2)}, u32[]{:S(2)}) %collective-permute-start.1) | collective-permute-done | bytes 524320 | tf_op jit(solution)/shard_map/while/body/ppermute | solution.py:59
  41.4 2.9 %collective-permute-start.2 = (f32[16,8,512]{2,1,0:T(8,128)S(1)}, f32[16,8,512]{2,1,0:T(8,128)S(1)}, u32[]{:S(2)}, u32[]{:S(2)}) collective-permute-start(f32[16,8,512]{2,1,0:T(8,128)S(1)} %slice.160), channel_id=1, source_target_pairs={{0,24},{1,97},{2,26},{3,99},{4,28},{5,101},{6,30},{7,103},{8,0},{9... | collective-permute-start | bytes 786440 | tf_op jit(solution)/shard_map/while/body/ppermute | solution.py:59
  44.5 3.2 %collective-permute-done.2 = f32[16,8,512]{2,1,0:T(8,128)S(1)} collective-permute-done((f32[16,8,512]{2,1,0:T(8,128)S(1)}, f32[16,8,512]{2,1,0:T(8,128)S(1)}, u32[]{:S(2)}, u32[]{:S(2)}) %collective-permute-start.2) | collective-permute-done | bytes 262176 | tf_op jit(solution)/shard_map/while/body/ppermute | solution.py:59
  47.7 3.2 %collective-permute-done.3 = f32[16,8,512]{2,1,0:T(8,128)S(1)} collective-permute-done((f32[16,8,512]{2,1,0:T(8,128)S(1)}, f32[16,8,512]{2,1,0:T(8,128)S(1)}, u32[]{:S(2)}, u32[]{:S(2)}) %collective-permute-start.3) | collective-permute-done | bytes 262176 | tf_op jit(solution)/shard_map/while/body/ppermute | solution.py:59
  53.3 1.7 collective-permute-start.5
  55.0 23.7 %collective-permute-done.4.before = f32[4,32,8,512]{3,2,1,0:T(8,128)S(1)} collective-permute-done((f32[4,32,8,512]{3,2,1,0:T(8,128)S(1)}, f32[4,32,8,512]{3,2,1,0:T(8,128)S(1)}, u32[]{:S(2)}, u32[]{:S(2)}) %collective-permute-start.4) | collective-permute-done | bytes 2097184 | tf_op jit(solution)/shard_map/while/body/ppermute | solution.py:59
  82.1 2.7 %collective-permute-start.7 = (f32[2,32,8,512]{3,2,1,0:T(8,128)}, f32[2,32,8,512]{3,2,1,0:T(8,128)}, u32[]{:S(2)}, u32[]{:S(2)}) collective-permute-start(f32[2,32,8,512]{3,2,1,0:T(8,128)} %slice.163), channel_id=1, source_target_pairs={{0,96},{1,25},{2,98},{3,27},{4,100},{5,29},{6,102},{7,31},{8,104},... | collective-permute-start | bytes 3145736 | tf_op jit(solution)/shard_map/while/body/ppermute | solution.py:59
  84.8 11.7 %collective-permute-done.6.far_low = f32[2,32,8,512]{3,2,1,0:T(8,128)} collective-permute-done((f32[2,32,8,512]{3,2,1,0:T(8,128)}, f32[2,32,8,512]{3,2,1,0:T(8,128)}, u32[]{:S(2)}, u32[]{:S(2)}) %collective-permute-start.6) | collective-permute-done | bytes 1048608 | tf_op jit(solution)/shard_map/while/body/ppermute | solution.py:59
  96.8 10.6 %tile_products.3 = (f32[2,10,128,512]{3,2,1,0:T(8,128)}, f32[4,160,1024]{2,1,0:T(8,128)}, f32[4,160,1024]{2,1,0:T(8,128)}) custom-call(s32[1]{0:T(128)} %bitcast.123.turn, s32[2,160]{1,0:T(2,128)S(1)} %get-tuple-element.277.structure, bf16[20,10,128,256]{3,2,1,0:T(8,128)(2,1)} %bitcast.128, ...), custom_call_target="tpu_custom_call", output_to_operand_aliasing={{0}: (8, {}), {1}: (9, {}), {2}: (10, {})} | custom-call | tf_op jit(solution)/shard_map/while/body/tile_products/pallas_call | solution.py:334
  107.4 3.6 %collective-permute-start.10 = (f32[4,160,1024]{2,1,0:T(8,128)}, f32[4,160,1024]{2,1,0:T(8,128)}, u32[]{:S(2)}, u32[]{:S(2)}) collective-permute-start(f32[4,160,1024]{2,1,0:T(8,128)} %get-tuple-element.126), channel_id=1, source_target_pairs={{0,1},{1,0},{2,3},{3,2},{4,5},{5,4},{6,7},{7,6},{8,9},{9,8},{10,11... | collective-permute-start | bytes 7864328 | tf_op jit(solution)/shard_map/ppermute | solution.py:457
  111.0 3.3 %fusion.32 = (f32[1,10,128,512]{3,2,1,0:T(8,128)S(1)}, f32[1,10,128,512]{3,2,1,0:T(8,128)S(1)}) fusion(f32[2,10,128,512]{3,2,1,0:T(8,128)} %get-tuple-element.127), kind=kLoop, calls=%fused_computation.87 | loop fusion | bytes 10485760 | tf_op jit(solution)/shard_map/slice | solution.py:441
  114.4 2.4 %fusion.35 = f32[512,512]{1,0:T(8,128)S(1)} fusion(f32[1280,512]{1,0:T(8,128)S(1)} %bitcast.133, f32[1280,512]{1,0:T(8,128)S(1)} %copy-done.5), kind=kOutput, calls=%fused_computation.90 | convolution fusion | flops 2013265920 | bytes 6291456 | tf_op jit(solution)/shard_map/dot_general | solution.py:67
  116.7 2.5 %fusion = f32[512,512]{0,1:T(8,128)S(1)} fusion(f32[1280,512]{1,0:T(8,128)S(1)} %bitcast.134, f32[1280,512]{1,0:T(8,128)S(1)} %copy-done.4, pred[1280]{0:T(1024)(128)(4,1)S(1)} %fusion.21), kind=kOutput, calls=%fused_computation.6 | convolution fusion | flops 2013921280 | bytes 6292736 | tf_op jit(solution)/shard_map/dot_general | solution.py:67
  122.4 2.4 %fusion.2 = f32[512,512]{0,1:T(8,128)S(1)} fusion(f32[512,512]{0,1:T(8,128)S(1)} %convolution_subtract_fusion, f32[1280,512]{1,0:T(8,128)S(1)} %bitcast.137, f32[1280,512]{1,0:T(8,128)S(1)} %copy-done.4), kind=kOutput, calls=%fused_computation.11 | convolution fusion | flops 2013528064 | bytes 7340032 | tf_op jit(solution)/shard_map/dot_general | solution.py:67
  126.4 3.7 %collective-permute-done.11 = f32[512,768]{0,1:T(8,128)} collective-permute-done((f32[512,768]{0,1:T(8,128)}, f32[512,768]{0,1:T(8,128)}, u32[]{:S(2)}, u32[]{:S(2)}) %collective-permute-start.11) | collective-permute-done | bytes 1572896 | tf_op jit(solution)/shard_map/ppermute | solution.py:380
  130.1 2.9 %maximum_add_fusion = f32[512,768]{0,1:T(8,128)} fusion(f32[512,768]{0,1:T(8,128)} %collective-permute-done.11, f32[512,256]{0,1:T(8,128)S(1)} %get-tuple-element.166, f32[512,256]{0,1:T(8,128)S(1)} %get-tuple-element.183, f32[512,256]{0,1:T(8,128)S(1)} %get-tuple-element.162), kind=kLoop, calls=%fused_computation.8 | loop fusion | flops 1179648 | bytes 4718592 | tf_op jit(solution)/shard_map/add | solution.py:381
  133.0 1.9 copy.26
  136.0 2.7 %collective-permute-start.14 = (f32[4,4,8,768]{3,2,1,0:T(8,128)}, f32[4,4,8,768]{3,2,1,0:T(8,128)}, u32[]{:S(2)}, u32[]{:S(2)}) collective-permute-start(f32[4,4,8,768]{3,2,1,0:T(8,128)} %get-tuple-element.161), channel_id=1, source_target_pairs={{0,96},{1,25},{2,98},{3,27},{4,100},{5,29},{6,102},{7,31},{8,104},... | collective-permute-start | bytes 1179656 | tf_op jit(solution)/shard_map/ppermute | solution.py:59
  138.7 3.1 %add.323 = f32[4,160,1024]{2,1,0:T(8,128)S(1)} add(f32[4,160,1024]{2,1,0:T(8,128)} %get-tuple-element.125, f32[4,160,1024]{2,1,0:T(8,128)} %collective-permute-done.10) | non-fusion elementwise | flops 655360 | bytes 7864320 | tf_op jit(solution)/shard_map/add | solution.py:457
  141.9 6.3 %collective-permute-start.21 = (f32[80,1024]{1,0:T(8,128)S(1)}, f32[80,1024]{1,0:T(8,128)S(1)}, u32[]{:S(2)}, u32[]{:S(2)}) collective-permute-start(f32[80,1024]{1,0:T(8,128)S(1)} %get-tuple-element.156), channel_id=1, source_target_pairs={{0,2},{1,3},{2,4},{3,5},{4,6},{5,7},{6,0},{7,1},{8,10},{9,11},{10,... | collective-permute-start | bytes 983048 | tf_op jit(solution)/shard_map/ppermute | solution.py:59
  148.3 5.9 %collective-permute-start.23 = (f32[80,1024]{1,0:T(8,128)S(1)}, f32[80,1024]{1,0:T(8,128)S(1)}, u32[]{:S(2)}, u32[]{:S(2)}) collective-permute-start(f32[80,1024]{1,0:T(8,128)S(1)} %get-tuple-element.154), channel_id=1, source_target_pairs={{0,6},{1,7},{2,0},{3,1},{4,2},{5,3},{6,4},{7,5},{8,14},{9,15},{10,... | collective-permute-start | bytes 983048 | tf_op jit(solution)/shard_map/ppermute | solution.py:59
  156.2 6.5 %collective-permute-start.16 = (f32[4,8,768]{2,1,0:T(8,128)S(1)}, f32[4,8,768]{2,1,0:T(8,128)S(1)}, u32[]{:S(2)}, u32[]{:S(2)}) collective-permute-start(f32[4,8,768]{2,1,0:T(8,128)S(1)} %get-tuple-element.170), channel_id=1, source_target_pairs={{0,16},{1,65},{2,18},{3,67},{4,20},{5,69},{6,22},{7,71},{8,24},{9,... | collective-permute-start | bytes 294920 | tf_op jit(solution)/shard_map/ppermute | solution.py:59
  163.8 7.0 %collective-permute-start.24 = (f32[160,1024]{1,0:T(8,128)}, f32[160,1024]{1,0:T(8,128)}, u32[]{:S(2)}, u32[]{:S(2)}) collective-permute-start(f32[160,1024]{1,0:T(8,128)} %pad_maximum_fusion.3), channel_id=1, source_target_pairs={{0,6},{1,7},{2,0},{3,1},{4,2},{5,3},{6,4},{7,5},{8,14},{9,15},{10,... | collective-permute-start | bytes 1966088 | tf_op jit(solution)/shard_map/ppermute | solution.py:59
  171.8 3.8 %collective-permute-start.19 = (f32[8,768]{1,0:T(8,128)S(1)}, f32[8,768]{1,0:T(8,128)S(1)}, u32[]{:S(2)}, u32[]{:S(2)}) collective-permute-start(f32[8,768]{1,0:T(8,128)S(1)} %get-tuple-element.173), channel_id=1, source_target_pairs={{0,4},{1,5},{2,6},{3,7},{4,0},{5,1},{6,2},{7,3},{8,12},{9,13},{10,... | collective-permute-start | bytes 73736 | tf_op jit(solution)/shard_map/ppermute | solution.py:59
  176.8 11.9 %collective-permute-done.18 = f32[8,768]{1,0:T(8,128)S(1)} collective-permute-done((f32[8,768]{1,0:T(8,128)S(1)}, f32[8,768]{1,0:T(8,128)S(1)}, u32[]{:S(2)}, u32[]{:S(2)}) %collective-permute-start.18) | collective-permute-done | bytes 24608 | tf_op jit(solution)/shard_map/ppermute | solution.py:59
  188.7 2.7 %collective-permute-start.25 = (f32[4,768]{1,0:T(4,128)S(1)}, f32[4,768]{1,0:T(4,128)S(1)}, u32[]{:S(2)}, u32[]{:S(2)}) collective-permute-start(f32[4,768]{1,0:T(4,128)S(1)} %slice_select_fusion), channel_id=1, source_target_pairs={{0,1},{1,0},{2,3},{3,2},{4,5},{5,4},{6,7},{7,6},{8,9},{9,8},{10,11... | collective-permute-start | bytes 36872 | tf_op jit(solution)/shard_map/ppermute | solution.py:396
  195.5 1.8 maximum_add_fusion.3
  (95 shorter events, 25.3 us)
Async XLA Ops:
  0.6 118.7 %copy-start = (f32[512,512]{1,0:T(8,128)S(1)}, f32[512,512]{1,0:T(8,128)}, u32[]{:S(2)}) copy-start(f32[512,512]{1,0:T(8,128)} %param.12) | copy-start | bytes 3145732
  0.8 14.5 %copy-start.9 = (s32[2,160]{1,0:T(2,128)S(1)}, s32[2,160]{1,0:T(2,128)}, u32[]{:S(2)}) copy-start(s32[2,160]{1,0:T(2,128)} %param.15) | copy-start | bytes 3844
  2.1 28.2 %collective-permute-start.8 = (f32[2,10,8,512]{3,2,1,0:T(8,128)S(1)}, f32[2,10,8,512]{3,2,1,0:T(8,128)S(1)}, u32[]{:S(2)}, u32[]{:S(2)}) collective-permute-start(f32[2,10,8,512]{3,2,1,0:T(8,128)S(1)} %get-tuple-element.152), channel_id=1, source_target_pairs={{0,0},{1,80},{2,8},{3,88},{4,16},{5,64},{6,24},{7,72},{8,48},{9,96... | collective-permute-start | bytes 983048 | tf_op jit(solution)/shard_map/ppermute | solution.py:422
  10.8 19.5 %collective-permute-start.9 = (f32[2,10,8,512]{3,2,1,0:T(8,128)S(1)}, f32[2,10,8,512]{3,2,1,0:T(8,128)}, u32[]{:S(2)}, u32[]{:S(2)}) collective-permute-start(f32[2,10,8,512]{3,2,1,0:T(8,128)S(1)} %get-tuple-element.151), channel_id=1, source_target_pairs={{0,40},{1,120},{2,48},{3,96},{4,56},{5,104},{6,32},{7,112},{8,8},{... | collective-permute-start | bytes 983048 | tf_op jit(solution)/shard_map/ppermute | solution.py:423
  32.9 8.5 %collective-permute-start.1 = (f32[32,8,512]{2,1,0:T(8,128)}, f32[32,8,512]{2,1,0:T(8,128)S(1)}, u32[]{:S(2)}, u32[]{:S(2)}) collective-permute-start(f32[32,8,512]{2,1,0:T(8,128)} %compact.3), channel_id=1, source_target_pairs={{0,24},{1,97},{2,26},{3,99},{4,28},{5,101},{6,30},{7,103},{8,0},{9... | collective-permute-start | bytes 1572872 | tf_op jit(solution)/shard_map/while/body/ppermute | solution.py:59
  34.5 9.8 %collective-permute-start = (f32[32,8,512]{2,1,0:T(8,128)}, f32[32,8,512]{2,1,0:T(8,128)S(1)}, u32[]{:S(2)}, u32[]{:S(2)}) collective-permute-start(f32[32,8,512]{2,1,0:T(8,128)} %compact.3), channel_id=1, source_target_pairs={{0,8},{1,33},{2,10},{3,35},{4,12},{5,37},{6,14},{7,39},{8,16},{9,4... | collective-permute-start | bytes 1572872 | tf_op jit(solution)/shard_map/while/body/ppermute | solution.py:59
  41.4 6.3 %collective-permute-start.2 = (f32[16,8,512]{2,1,0:T(8,128)S(1)}, f32[16,8,512]{2,1,0:T(8,128)S(1)}, u32[]{:S(2)}, u32[]{:S(2)}) collective-permute-start(f32[16,8,512]{2,1,0:T(8,128)S(1)} %slice.160), channel_id=1, source_target_pairs={{0,24},{1,97},{2,26},{3,99},{4,28},{5,101},{6,30},{7,103},{8,0},{9... | collective-permute-start | bytes 786440 | tf_op jit(solution)/shard_map/while/body/ppermute | solution.py:59
  44.4 6.5 %collective-permute-start.3 = (f32[16,8,512]{2,1,0:T(8,128)S(1)}, f32[16,8,512]{2,1,0:T(8,128)S(1)}, u32[]{:S(2)}, u32[]{:S(2)}) collective-permute-start(f32[16,8,512]{2,1,0:T(8,128)S(1)} %slice.161), channel_id=1, source_target_pairs={{0,8},{1,33},{2,10},{3,35},{4,12},{5,37},{6,14},{7,39},{8,16},{9,4... | collective-permute-start | bytes 786440 | tf_op jit(solution)/shard_map/while/body/ppermute | solution.py:59
  52.2 44.6 %copy-start.1 = (f32[4,32,8,512]{3,2,1,0:T(8,128)}, f32[4,32,8,512]{3,2,1,0:T(8,128)S(1)}, u32[]{:S(2)}) copy-start(f32[4,32,8,512]{3,2,1,0:T(8,128)S(1)} %pad_maximum_fusion.5.own) | copy-start | bytes 6291460 | tf_op jit(solution)/shard_map/while
  52.2 26.5 %collective-permute-start.4 = (f32[4,32,8,512]{3,2,1,0:T(8,128)S(1)}, f32[4,32,8,512]{3,2,1,0:T(8,128)S(1)}, u32[]{:S(2)}, u32[]{:S(2)}) collective-permute-start(f32[4,32,8,512]{3,2,1,0:T(8,128)S(1)} %pad_maximum_fusion.5.own), channel_id=1, source_target_pairs={{0,32},{1,9},{2,34},{3,11},{4,36},{5,13},{6,38},{7,15},{8,40},{9,1... | collective-permute-start | bytes 6291464 | tf_op jit(solution)/shard_map/while/body/ppermute | solution.py:59
  53.3 25.4 %collective-permute-start.5 = (f32[4,32,8,512]{3,2,1,0:T(8,128)S(1)}, f32[4,32,8,512]{3,2,1,0:T(8,128)S(1)}, u32[]{:S(2)}, u32[]{:S(2)}) collective-permute-start(f32[4,32,8,512]{3,2,1,0:T(8,128)S(1)} %pad_maximum_fusion.5.own), channel_id=1, source_target_pairs={{0,96},{1,25},{2,98},{3,27},{4,100},{5,29},{6,102},{7,31},{8,104},... | collective-permute-start | bytes 6291464 | tf_op jit(solution)/shard_map/while/body/ppermute | solution.py:59
  81.0 15.5 %collective-permute-start.6 = (f32[2,32,8,512]{3,2,1,0:T(8,128)}, f32[2,32,8,512]{3,2,1,0:T(8,128)}, u32[]{:S(2)}, u32[]{:S(2)}) collective-permute-start(f32[2,32,8,512]{3,2,1,0:T(8,128)} %slice.162), channel_id=1, source_target_pairs={{0,32},{1,9},{2,34},{3,11},{4,36},{5,13},{6,38},{7,15},{8,40},{9,1... | collective-permute-start | bytes 3145736 | tf_op jit(solution)/shard_map/while/body/ppermute | solution.py:59
  82.1 14.7 %collective-permute-start.7 = (f32[2,32,8,512]{3,2,1,0:T(8,128)}, f32[2,32,8,512]{3,2,1,0:T(8,128)}, u32[]{:S(2)}, u32[]{:S(2)}) collective-permute-start(f32[2,32,8,512]{3,2,1,0:T(8,128)} %slice.163), channel_id=1, source_target_pairs={{0,96},{1,25},{2,98},{3,27},{4,100},{5,29},{6,102},{7,31},{8,104},... | collective-permute-start | bytes 3145736 | tf_op jit(solution)/shard_map/while/body/ppermute | solution.py:59
  107.4 31.3 %collective-permute-start.10 = (f32[4,160,1024]{2,1,0:T(8,128)}, f32[4,160,1024]{2,1,0:T(8,128)}, u32[]{:S(2)}, u32[]{:S(2)}) collective-permute-start(f32[4,160,1024]{2,1,0:T(8,128)} %get-tuple-element.126), channel_id=1, source_target_pairs={{0,1},{1,0},{2,3},{3,2},{4,5},{5,4},{6,7},{7,6},{8,9},{9,8},{10,11... | collective-permute-start | bytes 7864328 | tf_op jit(solution)/shard_map/ppermute | solution.py:457
  126.4 3.8 %collective-permute-start.11 = (f32[512,768]{0,1:T(8,128)}, f32[512,768]{0,1:T(8,128)}, u32[]{:S(2)}, u32[]{:S(2)}) collective-permute-start(f32[512,768]{0,1:T(8,128)} %pad_maximum_fusion.1), channel_id=1, source_target_pairs={{0,1},{1,0},{2,3},{3,2},{4,5},{5,4},{6,7},{7,6},{8,9},{9,8},{10,11... | collective-permute-start | bytes 4718600 | tf_op jit(solution)/shard_map/ppermute | solution.py:380
  136.0 18.2 %collective-permute-start.12 = (f32[4,4,8,768]{3,2,1,0:T(8,128)}, f32[4,4,8,768]{3,2,1,0:T(8,128)S(1)}, u32[]{:S(2)}, u32[]{:S(2)}) collective-permute-start(f32[4,4,8,768]{3,2,1,0:T(8,128)} %get-tuple-element.159), channel_id=1, source_target_pairs={{0,32},{1,9},{2,34},{3,11},{4,36},{5,13},{6,38},{7,15},{8,40},{9,1... | collective-permute-start | bytes 1179656 | tf_op jit(solution)/shard_map/ppermute | solution.py:59
  136.0 18.2 %collective-permute-start.13 = (f32[4,4,8,768]{3,2,1,0:T(8,128)}, f32[4,4,8,768]{3,2,1,0:T(8,128)S(1)}, u32[]{:S(2)}, u32[]{:S(2)}) collective-permute-start(f32[4,4,8,768]{3,2,1,0:T(8,128)} %get-tuple-element.160), channel_id=1, source_target_pairs={{0,64},{1,17},{2,66},{3,19},{4,68},{5,21},{6,70},{7,23},{8,72},{9,... | collective-permute-start | bytes 1179656 | tf_op jit(solution)/shard_map/ppermute | solution.py:59
  136.0 18.2 %collective-permute-start.14 = (f32[4,4,8,768]{3,2,1,0:T(8,128)}, f32[4,4,8,768]{3,2,1,0:T(8,128)}, u32[]{:S(2)}, u32[]{:S(2)}) collective-permute-start(f32[4,4,8,768]{3,2,1,0:T(8,128)} %get-tuple-element.161), channel_id=1, source_target_pairs={{0,96},{1,25},{2,98},{3,27},{4,100},{5,29},{6,102},{7,31},{8,104},... | collective-permute-start | bytes 1179656 | tf_op jit(solution)/shard_map/ppermute | solution.py:59
  141.8 20.9 %copy-start.6 = (f32[4,160,1024]{2,1,0:T(8,128)}, f32[4,160,1024]{2,1,0:T(8,128)S(1)}, u32[]{:S(2)}) copy-start(f32[4,160,1024]{2,1,0:T(8,128)S(1)} %add.323) | copy-start | bytes 7864324
  141.9 20.8 %collective-permute-start.21 = (f32[80,1024]{1,0:T(8,128)S(1)}, f32[80,1024]{1,0:T(8,128)S(1)}, u32[]{:S(2)}, u32[]{:S(2)}) collective-permute-start(f32[80,1024]{1,0:T(8,128)S(1)} %get-tuple-element.156), channel_id=1, source_target_pairs={{0,2},{1,3},{2,4},{3,5},{4,6},{5,7},{6,0},{7,1},{8,10},{9,11},{10,... | collective-permute-start | bytes 983048 | tf_op jit(solution)/shard_map/ppermute | solution.py:59
  148.3 14.5 %collective-permute-start.23 = (f32[80,1024]{1,0:T(8,128)S(1)}, f32[80,1024]{1,0:T(8,128)S(1)}, u32[]{:S(2)}, u32[]{:S(2)}) collective-permute-start(f32[80,1024]{1,0:T(8,128)S(1)} %get-tuple-element.154), channel_id=1, source_target_pairs={{0,6},{1,7},{2,0},{3,1},{4,2},{5,3},{6,4},{7,5},{8,14},{9,15},{10,... | collective-permute-start | bytes 983048 | tf_op jit(solution)/shard_map/ppermute | solution.py:59
  155.4 16.3 %collective-permute-start.15 = (f32[4,8,768]{2,1,0:T(8,128)S(1)}, f32[4,8,768]{2,1,0:T(8,128)S(1)}, u32[]{:S(2)}, u32[]{:S(2)}) collective-permute-start(f32[4,8,768]{2,1,0:T(8,128)S(1)} %get-tuple-element.168), channel_id=1, source_target_pairs={{0,8},{1,33},{2,10},{3,35},{4,12},{5,37},{6,14},{7,39},{8,16},{9,4... | collective-permute-start | bytes 294920 | tf_op jit(solution)/shard_map/ppermute | solution.py:59
  156.2 15.5 %collective-permute-start.16 = (f32[4,8,768]{2,1,0:T(8,128)S(1)}, f32[4,8,768]{2,1,0:T(8,128)S(1)}, u32[]{:S(2)}, u32[]{:S(2)}) collective-permute-start(f32[4,8,768]{2,1,0:T(8,128)S(1)} %get-tuple-element.170), channel_id=1, source_target_pairs={{0,16},{1,65},{2,18},{3,67},{4,20},{5,69},{6,22},{7,71},{8,24},{9,... | collective-permute-start | bytes 294920 | tf_op jit(solution)/shard_map/ppermute | solution.py:59
  162.7 12.9 %copy-start.8 = (f32[512,512]{1,0:T(8,128)S(1)}, f32[512,512]{1,0:T(8,128)}, u32[]{:S(2)}) copy-start(f32[512,512]{1,0:T(8,128)} %param.13) | copy-start | bytes 3145732
  162.7 8.9 %collective-permute-start.17 = (f32[4,8,768]{2,1,0:T(8,128)S(1)}, f32[4,8,768]{2,1,0:T(8,128)S(1)}, u32[]{:S(2)}, u32[]{:S(2)}) collective-permute-start(f32[4,8,768]{2,1,0:T(8,128)S(1)} %get-tuple-element.169), channel_id=1, source_target_pairs={{0,24},{1,97},{2,26},{3,99},{4,28},{5,101},{6,30},{7,103},{8,0},{9... | collective-permute-start | bytes 294920 | tf_op jit(solution)/shard_map/ppermute | solution.py:59
  163.8 25.0 %collective-permute-start.24 = (f32[160,1024]{1,0:T(8,128)}, f32[160,1024]{1,0:T(8,128)}, u32[]{:S(2)}, u32[]{:S(2)}) collective-permute-start(f32[160,1024]{1,0:T(8,128)} %pad_maximum_fusion.3), channel_id=1, source_target_pairs={{0,6},{1,7},{2,0},{3,1},{4,2},{5,3},{6,4},{7,5},{8,14},{9,15},{10,... | collective-permute-start | bytes 1966088 | tf_op jit(solution)/shard_map/ppermute | solution.py:59
  171.6 17.1 %collective-permute-start.22 = (f32[160,1024]{1,0:T(8,128)}, f32[160,1024]{1,0:T(8,128)}, u32[]{:S(2)}, u32[]{:S(2)}) collective-permute-start(f32[160,1024]{1,0:T(8,128)} %pad_maximum_fusion.2), channel_id=1, source_target_pairs={{0,2},{1,3},{2,4},{3,5},{4,6},{5,7},{6,0},{7,1},{8,10},{9,11},{10,... | collective-permute-start | bytes 1966088 | tf_op jit(solution)/shard_map/ppermute | solution.py:59
  171.7 17.0 %collective-permute-start.18 = (f32[8,768]{1,0:T(8,128)S(1)}, f32[8,768]{1,0:T(8,128)S(1)}, u32[]{:S(2)}, u32[]{:S(2)}) collective-permute-start(f32[8,768]{1,0:T(8,128)S(1)} %get-tuple-element.171), channel_id=1, source_target_pairs={{0,2},{1,3},{2,4},{3,5},{4,6},{5,7},{6,0},{7,1},{8,10},{9,11},{10,... | collective-permute-start | bytes 73736 | tf_op jit(solution)/shard_map/ppermute | solution.py:59
  171.8 16.9 %collective-permute-start.19 = (f32[8,768]{1,0:T(8,128)S(1)}, f32[8,768]{1,0:T(8,128)S(1)}, u32[]{:S(2)}, u32[]{:S(2)}) collective-permute-start(f32[8,768]{1,0:T(8,128)S(1)} %get-tuple-element.173), channel_id=1, source_target_pairs={{0,4},{1,5},{2,6},{3,7},{4,0},{5,1},{6,2},{7,3},{8,12},{9,13},{10,... | collective-permute-start | bytes 73736 | tf_op jit(solution)/shard_map/ppermute | solution.py:59
  175.6 13.1 %collective-permute-start.20 = (f32[8,768]{1,0:T(8,128)S(1)}, f32[8,768]{1,0:T(8,128)S(1)}, u32[]{:S(2)}, u32[]{:S(2)}) collective-permute-start(f32[8,768]{1,0:T(8,128)S(1)} %get-tuple-element.172), channel_id=1, source_target_pairs={{0,6},{1,7},{2,0},{3,1},{4,2},{5,3},{6,4},{7,5},{8,14},{9,15},{10,... | collective-permute-start | bytes 73736 | tf_op jit(solution)/shard_map/ppermute | solution.py:59
  188.7 5.5 %collective-permute-start.25 = (f32[4,768]{1,0:T(4,128)S(1)}, f32[4,768]{1,0:T(4,128)S(1)}, u32[]{:S(2)}, u32[]{:S(2)}) collective-permute-start(f32[4,768]{1,0:T(4,128)S(1)} %slice_select_fusion), channel_id=1, source_target_pairs={{0,1},{1,0},{2,3},{3,2},{4,5},{5,4},{6,7},{7,6},{8,9},{9,8},{10,11... | collective-permute-start | bytes 36872 | tf_op jit(solution)/shard_map/ppermute | solution.py:396
  193.0 4.3 %copy-start.7 = (f32[160,512]{1,0:T(8,128)}, f32[160,512]{1,0:T(8,128)S(1)}, u32[]{:S(2)}) copy-start(f32[160,512]{1,0:T(8,128)S(1)} %slice_negate_fusion) | copy-start | bytes 983044
  (4 other events, 9.4 us)
where the time goes:
time: 198 us; the launch traced here: 197 us
  waiting for transfers between devices  64.8 us (33%)
  starting transfers between devices  62.7 us (32%)
  Pallas kernels  26.4 us (13%)
  other arithmetic  17.9 us (9%)
  matrix products  14.4 us (7%)
  local copies, waits for them, and re-layouts  9.22 us (5%)
    ppermute x21, waiting for transfers between devices, shift(): return lax.ppermute(value, AXES, stepped(axis, by))  61 us
    ppermute x21, starting transfers between devices, shift(): return lax.ppermute(value, AXES, stepped(axis, by))  43.3 us
    pallas_call x1, Pallas kernels, narrow(): pl.pallas_call(narrow_body, grid=(TILE_BLOCKS,), in_specs=[pl.BlockSpec((...  13.2 us
    dot_general x6, matrix products, product_t(): lax.dot_general(left, right, (((0,), (0,)), ((), ())), precision=lax.Prec...  11.1 us
    pallas_call x1, Pallas kernels, tile_products(): pl.pallas_call(tile_body, in_specs=[smem, smem] + [hbm] * 9, out_specs=[h...  10.6 us
    ppermute x1, starting transfers between devices, invert(): first = lax.ppermute(slices(0), AXES, SPREAD[0])  8.66 us
    ppermute x1, starting transfers between devices, invert(): second = lax.ppermute(slices(1), AXES, SPREAD[1])  4.51 us
  transfers between devices with their start and end apart: 26, of which 8 were waited for; matrix products, arithmetic and copies ran while one was open for 17% of the time, Pallas kernels for 7%

commit v1 on v0

--- a/solution.py
+++ b/solution.py
@@ -1,3 +1,5 @@
+import itertools
+
 import jax
 import jax.numpy as jnp
 from jax import lax
@@ -17,7 +19,8 @@
 W = 512
 AXES = ("row", "col")
 SLOTS = 32
-CHUNKS = ((0, 6), (6, 10))
+FEW = 6
+EARLY = SLOTS // 2
 
 
 def device(y, x, z, core):
@@ -166,13 +169,14 @@
     pieces += [(far_low, 2, i, i) for i in range(2)]
     pieces += [(far_high, 2, i, i + 2) for i in range(2)]
     copies = []
-    for ref, outer, at, inner in pieces:
+    for half, (ref, outer, at, inner) in itertools.product(range(2), pieces):
+        span = pl.ds(half * EARLY, EARLY)
         sub_y = (y + jnp.where(core == 0, outer, inner)) % SIDE
         sub_x = (x + jnp.where(core == 0, inner, outer)) % SIDE
         copies.append(
             pltpu.make_async_copy(
-                ref.at[at],
-                panel.at[pl.ds(0, SLOTS), sub_y * SIDE + sub_x],
+                ref.at[at, span],
+                panel.at[span, sub_y * SIDE + sub_x],
                 panel_sem.at[len(copies)],
             )
         )
@@ -259,7 +263,7 @@
         old.wait()
 
     panel[SLOTS] = jnp.zeros((BLK // SUB, SUB, W), jnp.float32)
-    for copy in copies:
+    for copy in copies[: len(pieces)]:
         copy.wait()
 
     def contract(which, lines, step):
@@ -274,11 +278,11 @@
             right[pl.ds((2 * at + 1) * BLK, BLK)] = high
             right[pl.ds((4 + at) * BLK, BLK)] = low
 
-        for begin, stop in CHUNKS:
-
-            @pl.when(lines > begin)
+        for stop, chosen in ((FEW, lines <= FEW), (TILE_BLOCKS, lines > FEW)):
+
+            @pl.when(chosen)
             def _():
-                picked = [rows[which, at] for at in range(begin, stop)]
+                picked = [rows[which, at] for at in range(stop)]
                 value = jnp.concatenate(
                     [left[buffer, jnp.minimum(at, TILE_BLOCKS - 1)] for at in picked], axis=0
                 )
@@ -318,7 +322,11 @@
         contract(1, child_lines, step)
         return 0
 
-    lax.fori_loop(0, parent_steps, parent_step, 0)
+    early_steps = jnp.minimum(parent_steps, EARLY // 2)
+    lax.fori_loop(0, early_steps, parent_step, 0)
+    for copy in copies[len(pieces) :]:
+        copy.wait()
+    lax.fori_loop(early_steps, parent_steps, parent_step, 0)
     for copy in out_copies[0]:
         copy.start()
     lax.fori_loop(parent_steps, steps, child_step, 0)
@@ -344,7 +352,7 @@
             pltpu.VMEM((SLOTS + 1, BLK // SUB, SUB, W), jnp.float32),
             pltpu.VMEM((6 * BLK, W), jnp.bfloat16),
             pltpu.VMEM((2, TILE_BLOCKS + 1, BLK, W), jnp.float32),
-            pltpu.SemaphoreType.DMA((16,)),
+            pltpu.SemaphoreType.DMA((32,)),
             pltpu.SemaphoreType.DMA((2, 2)),
             pltpu.SemaphoreType.DMA((18,)),
         ],
@@ -365,6 +373,30 @@
     return piece(0) + got[0] + got[1] + got[2]
 
 
+def finish_body(base, kept, got, parent_diag, child_top, child_diag):
+    half = W // CORES
+    first = lax.axis_index("col") % CORES == 0
+    left = jnp.where(first, kept[...], got[...])
+    right = jnp.where(first, got[...], kept[...])
+    for at, out in enumerate((parent_diag, child_top, child_diag)):
+        columns = slice(at * half, (at + 1) * half)
+        total = base[:, at * W : (at + 1) * W] + jnp.concatenate(
+            [left[:, columns], right[:, columns]], axis=1
+        )
+        out[...] = -total if at == 1 else total
+
+
+def finish(base, kept, got):
+    vmem = pl.BlockSpec(memory_space=pltpu.VMEM)
+    return pl.pallas_call(
+        finish_body,
+        in_specs=[vmem] * 3,
+        out_specs=[vmem] * 3,
+        out_shape=[jax.ShapeDtypeStruct((base.shape[0], W), jnp.float32)] * 3,
+        name="finish",
+    )(base, kept, got)
+
+
 def final_sums(terms, chunks, up, down, y, x, z, core):
     half = W // CORES
 
@@ -394,12 +426,7 @@
     low, high = value[: SUB // 2], value[SUB // 2 :]
     kept = jnp.where(core == 0, low, high)
     got = lax.ppermute(jnp.where(core == 0, high, low), AXES, PARTNER)
-    left, right = jnp.where(core == 0, kept, got), jnp.where(core == 0, got, kept)
-    sums = [
-        jnp.concatenate([part[:, at * half : (at + 1) * half] for part in (left, right)], axis=1)
-        for at in range(len(terms))
-    ]
-    return rows, sums
+    return rows, kept, got
 
 
 def invert(
@@ -424,19 +451,31 @@
     counts = structure.reshape(2, SIDE * CORES, COL_BLOCKS).sum(axis=(0, 2))
     turns = (jnp.max(counts) + SLOTS - 1) // SLOTS
 
+    def own_rows(values):
+        return lax.dynamic_slice_in_dim(values, own_start, own_count, 0)
+
+    def base_of(coupling, diag_parent, diag_child):
+        top = product(diag_parent, coupling)
+        columns = lax.dynamic_slice_in_dim(coupling, own_start, own_count, 1)
+        rest = own_rows(diag_child) + product_t(columns, top)
+        return jnp.concatenate([own_rows(diag_parent), own_rows(top), rest], axis=1)
+
     def one_turn(at, old):
         turn = jnp.reshape(at, (1,))
         share = compact(turn, structure, first, second)
+        share, *small = lax.optimization_barrier((share, coupling, diag_parent, diag_child))
         line = jnp.stack(gather_line(share, "xy"))
         near = gather_near(line, "yx")
-        near, parts = lax.optimization_barrier((near, narrow(ancestor_inverse)))
+        near, parts, base = lax.optimization_barrier(
+            (near, narrow(ancestor_inverse), base_of(*small))
+        )
         lines = (line, *near, *gather_far(*near, "yx"))
-        return tuple(tile_products(turn, structure, parts, lines, old))
+        return base, *tile_products(turn, structure, parts, lines, old[1:])
 
     start = tuple(
-        blank((2, TILE_BLOCKS, BLK, W), (SIDE, GROUP, 2 * W), (SIDE, GROUP, 2 * W))
-    )
-    whole, mine, theirs = lax.fori_loop(0, turns, one_turn, start)
+        blank((own_count, 3 * W), (2, TILE_BLOCKS, BLK, W), (SIDE, GROUP, 2 * W), (SIDE, GROUP, 2 * W))
+    )
+    base, whole, mine, theirs = lax.fori_loop(0, turns, one_turn, start)
     parent_whole = whole[0].reshape(tile_rows, W)
     child_whole = whole[1].reshape(tile_rows, W)
 
@@ -446,13 +485,6 @@
     mask_child = jnp.any(hits, axis=1)[:, None]
     child = jnp.where(mask_child, panel_child, 0)
     mask_group = lax.dynamic_slice_in_dim(mask_child, col * group_rows, group_rows, 0)
-
-    def own_rows(values):
-        return lax.dynamic_slice_in_dim(values, own_start, own_count, 0)
-
-    base_top = product(diag_parent, coupling)
-    coupling_cols = lax.dynamic_slice_in_dim(coupling, own_start, own_count, 1)
-    base_child = own_rows(diag_child) + product_t(coupling_cols, base_top)
 
     chunks = mine + lax.ppermute(theirs, AXES, PARTNER)
     cut = GROUP // 2
@@ -464,14 +496,12 @@
     child_term = (
         product_t(coupling, top_term) - product_t(cross, coupling) + product_t(panel_child, child_whole)
     )
-    rows, (parent_sum, top_sum, child_sum) = final_sums(
+    rows, kept, got = final_sums(
         [parent_term, top_term, child_term], chunks, up, down, y, x, z, core
     )
     parent_rows = -rows[:, :W]
     child_rows = -(rows[:, W:] + jnp.where(mask_group, product(parent_rows, coupling), 0))
-    parent_diag = own_rows(diag_parent) + parent_sum
-    child_top = -(own_rows(base_top) + top_sum)
-    child_diag = base_child + child_sum
+    parent_diag, child_top, child_diag = finish(base, kept, got)
     return parent_rows, parent_diag, child_top, child_rows, child_diag
 
 

time: 198 us -> 196 us (0.990)
  waiting for transfers between devices: 64.8 us -> 62.7 us
    ppermute x21, waiting for transfers between devices: 61 us -> 58.9 us  [shift(): return lax.ppermute(value, AXES, stepped(axis, by))]
where the time goes in v1:
time: 196 us; the launch traced here: 195 us
  waiting for transfers between devices  62.7 us (32%)
  starting transfers between devices  61.7 us (31%)
  Pallas kernels  27.9 us (14%)
  other arithmetic  17.5 us (9%)
  matrix products  13.8 us (7%)
  local copies, waits for them, and re-layouts  9.31 us (5%)
    ppermute x21, waiting for transfers between devices, shift(): return lax.ppermute(value, AXES, stepped(axis, by))  58.9 us
    ppermute x21, starting transfers between devices, shift(): return lax.ppermute(value, AXES, stepped(axis, by))  41.7 us
    pallas_call x1, Pallas kernels, narrow(): pl.pallas_call(narrow_body, grid=(TILE_BLOCKS,), in_specs=[pl.BlockSpec((...  13.2 us
    pallas_call x1, Pallas kernels, tile_products(): pl.pallas_call(tile_body, in_specs=[smem, smem] + [hbm] * 9, out_specs=[h...  10.8 us
    dot_general x6, matrix products, product_t(): lax.dot_general(left, right, (((0,), (0,)), ((), ())), precision=lax.Prec...  10.5 us
    ppermute x1, starting transfers between devices, invert(): first = lax.ppermute(slices(0), AXES, SPREAD[0])  8.66 us
    ppermute x1, starting transfers between devices, invert(): second = lax.ppermute(slices(1), AXES, SPREAD[1])  4.51 us
    ppermute x1, starting transfers between devices, invert(): chunks = mine + lax.ppermute(theirs, AXES, PARTNER)  4.02 us
  transfers between devices with their start and end apart: 26, of which 8 were waited for; matrix products, arithmetic and copies ran while one was open for 17% of the time, Pallas kernels for 7%

profile of v1, /device:TPU:1, one launch (start us, length us, event | category | flops | bytes accessed | tf_op | source)
XLA Modules:
  0.0 194.8 jit_solution(7903013283720219315)
XLA Ops:
  2.0 8.7 %collective-permute-start.8 = (f32[2,10,8,512]{3,2,1,0:T(8,128)S(1)}, f32[2,10,8,512]{3,2,1,0:T(8,128)S(1)}, u32[]{:S(2)}, u32[]{:S(2)}) collective-permute-start(f32[2,10,8,512]{3,2,1,0:T(8,128)S(1)} %get-tuple-element.236), channel_id=1, source_target_pairs={{0,0},{1,80},{2,8},{3,88},{4,16},{5,64},{6,24},{7,72},{8,48},{9,96... | collective-permute-start | bytes 983048 | tf_op jit(solution)/shard_map/ppermute | solution.py:449
  10.7 4.5 %collective-permute-start.9 = (f32[2,10,8,512]{3,2,1,0:T(8,128)S(1)}, f32[2,10,8,512]{3,2,1,0:T(8,128)}, u32[]{:S(2)}, u32[]{:S(2)}) collective-permute-start(f32[2,10,8,512]{3,2,1,0:T(8,128)S(1)} %get-tuple-element.235), channel_id=1, source_target_pairs={{0,40},{1,120},{2,48},{3,96},{4,56},{5,104},{6,32},{7,112},{8,8},{... | collective-permute-start | bytes 983048 | tf_op jit(solution)/shard_map/ppermute | solution.py:450
  16.8 13.2 %narrow.3 = bf16[20,1280,256]{2,1,0:T(8,128)(2,1)} custom-call(f32[1280,2560]{1,0:T(8,128)} %value), custom_call_target="tpu_custom_call" | custom-call | bytes 26214400 | tf_op jit(solution)/shard_map/while/body/narrow/pallas_call | solution.py:138
  30.2 76.4 %while.18 = (s32[]{:T(128)}, f32[4,1536]{1,0:T(4,128)}, f32[2,10,128,512]{3,2,1,0:T(8,128)}, f32[4,160,1024]{2,1,0:T(8,128)}, f32[4,160,1024]{2,1,0:T(8,128)}, /...) while((s32[]{:T(128)}, f32[4,1536]{1,0:T(4,128)}, ...), condition=%wide.region_4.5_spmd, body=%wide.region_3.4_spmd.sunk | while | flops 813316096 | bytes 75859528 | solution.py:478
  30.2 2.6 %compact.3 = f32[32,8,512]{2,1,0:T(8,128)} custom-call(s32[1]{0:T(128)} %bitcast.129.turn, s32[2,160]{1,0:T(2,128)S(1)} %get-tuple-element.406.structure, f32[2,10,8,512]{3,2,1,0:T(8,128)S(1)} %get-tuple-element.407.first, f32[2,10,8,512]{3,2,1,0:T(8,128)} %get-tuple-element.408.second), custom_call_target="tpu_custom_call" | custom-call | tf_op jit(solution)/shard_map/while/body/compact/pallas_call | solution.py:99
  32.8 1.7 collective-permute-start.1
  34.5 6.9 %collective-permute-done.1 = f32[32,8,512]{2,1,0:T(8,128)S(1)} collective-permute-done((f32[32,8,512]{2,1,0:T(8,128)}, f32[32,8,512]{2,1,0:T(8,128)S(1)}, u32[]{:S(2)}, u32[]{:S(2)}) %collective-permute-start.1) | collective-permute-done | bytes 524320 | tf_op jit(solution)/shard_map/while/body/ppermute | solution.py:62
  41.4 2.9 %collective-permute-start.2 = (f32[16,8,512]{2,1,0:T(8,128)S(1)}, f32[16,8,512]{2,1,0:T(8,128)S(1)}, u32[]{:S(2)}, u32[]{:S(2)}) collective-permute-start(f32[16,8,512]{2,1,0:T(8,128)S(1)} %slice.116), channel_id=1, source_target_pairs={{0,24},{1,97},{2,26},{3,99},{4,28},{5,101},{6,30},{7,103},{8,0},{9... | collective-permute-start | bytes 786440 | tf_op jit(solution)/shard_map/while/body/ppermute | solution.py:62
  44.5 3.2 %collective-permute-done.2 = f32[16,8,512]{2,1,0:T(8,128)S(1)} collective-permute-done((f32[16,8,512]{2,1,0:T(8,128)S(1)}, f32[16,8,512]{2,1,0:T(8,128)S(1)}, u32[]{:S(2)}, u32[]{:S(2)}) %collective-permute-start.2) | collective-permute-done | bytes 262176 | tf_op jit(solution)/shard_map/while/body/ppermute | solution.py:62
  47.7 3.2 %collective-permute-done.3 = f32[16,8,512]{2,1,0:T(8,128)S(1)} collective-permute-done((f32[16,8,512]{2,1,0:T(8,128)S(1)}, f32[16,8,512]{2,1,0:T(8,128)S(1)}, u32[]{:S(2)}, u32[]{:S(2)}) %collective-permute-start.3) | collective-permute-done | bytes 262176 | tf_op jit(solution)/shard_map/while/body/ppermute | solution.py:62
  53.2 1.7 collective-permute-start.5
  57.8 20.9 %collective-permute-done.4.before = f32[4,32,8,512]{3,2,1,0:T(8,128)S(1)} collective-permute-done((f32[4,32,8,512]{3,2,1,0:T(8,128)S(1)}, f32[4,32,8,512]{3,2,1,0:T(8,128)S(1)}, u32[]{:S(2)}, u32[]{:S(2)}) %collective-permute-start.4) | collective-permute-done | bytes 2097184 | tf_op jit(solution)/shard_map/while/body/ppermute | solution.py:62
  81.5 2.4 %collective-permute-start.7 = (f32[2,32,8,512]{3,2,1,0:T(8,128)}, f32[2,32,8,512]{3,2,1,0:T(8,128)}, u32[]{:S(2)}, u32[]{:S(2)}) collective-permute-start(f32[2,32,8,512]{3,2,1,0:T(8,128)} %slice.119), channel_id=1, source_target_pairs={{0,96},{1,25},{2,98},{3,27},{4,100},{5,29},{6,102},{7,31},{8,104},... | collective-permute-start | bytes 3145736 | tf_op jit(solution)/shard_map/while/body/ppermute | solution.py:62
  83.8 11.4 %collective-permute-done.6.far_low = f32[2,32,8,512]{3,2,1,0:T(8,128)} collective-permute-done((f32[2,32,8,512]{3,2,1,0:T(8,128)}, f32[2,32,8,512]{3,2,1,0:T(8,128)}, u32[]{:S(2)}, u32[]{:S(2)}) %collective-permute-start.6) | collective-permute-done | bytes 1048608 | tf_op jit(solution)/shard_map/while/body/ppermute | solution.py:62
  95.9 10.8 %tile_products.3 = (f32[2,10,128,512]{3,2,1,0:T(8,128)}, f32[4,160,1024]{2,1,0:T(8,128)}, f32[4,160,1024]{2,1,0:T(8,128)}) custom-call(s32[1]{0:T(128)} %bitcast.129.turn, s32[2,160]{1,0:T(2,128)S(1)} %get-tuple-element.406.structure, bf16[20,10,128,256]{3,2,1,0:T(8,128)(2,1)} %bitcast.134, ...), custom_call_target="tpu_custom_call", output_to_operand_aliasing={{0}: (8, {}), {1}: (9, {}), {2}: (10, {})} | custom-call | tf_op jit(solution)/shard_map/while/body/tile_products/pallas_call | solution.py:342
  106.6 4.0 %collective-permute-start.10 = (f32[4,160,1024]{2,1,0:T(8,128)}, f32[4,160,1024]{2,1,0:T(8,128)}, u32[]{:S(2)}, u32[]{:S(2)}) collective-permute-start(f32[4,160,1024]{2,1,0:T(8,128)} %get-tuple-element.194), channel_id=1, source_target_pairs={{0,1},{1,0},{2,3},{3,2},{4,5},{5,4},{6,7},{7,6},{8,9},{9,8},{10,11... | collective-permute-start | bytes 7864328 | tf_op jit(solution)/shard_map/ppermute | solution.py:489
  110.7 3.3 %fusion.29 = (f32[1,10,128,512]{3,2,1,0:T(8,128)S(1)}, f32[1,10,128,512]{3,2,1,0:T(8,128)S(1)}) fusion(f32[2,10,128,512]{3,2,1,0:T(8,128)} %get-tuple-element.195), kind=kLoop, calls=%fused_computation.84 | loop fusion | bytes 10485760 | tf_op jit(solution)/shard_map/slice | solution.py:480
  114.0 2.4 %fusion.31 = f32[512,512]{1,0:T(8,128)S(1)} fusion(f32[1280,512]{1,0:T(8,128)S(1)} %bitcast.139, f32[1280,512]{1,0:T(8,128)S(1)} %copy-done.6), kind=kOutput, calls=%fused_computation.86 | convolution fusion | flops 2013265920 | bytes 6291456 | tf_op jit(solution)/shard_map/dot_general | solution.py:70
  116.4 2.5 %fusion.2 = f32[512,512]{0,1:T(8,128)S(1)} fusion(f32[1280,512]{1,0:T(8,128)S(1)} %bitcast.140, f32[1280,512]{1,0:T(8,128)S(1)} %copy-done.5, pred[1280]{0:T(1024)(128)(4,1)S(1)} %fusion.22), kind=kOutput, calls=%fused_computation.12 | convolution fusion | flops 2013921280 | bytes 6292736 | tf_op jit(solution)/shard_map/dot_general | solution.py:70
  122.0 2.4 %fusion.4 = f32[512,512]{0,1:T(8,128)S(1)} fusion(f32[512,512]{0,1:T(8,128)S(1)} %convolution_subtract_fusion, f32[1280,512]{1,0:T(8,128)S(1)} %bitcast.143, f32[1280,512]{1,0:T(8,128)S(1)} %copy-done.5), kind=kOutput, calls=%fused_computation.17 | convolution fusion | flops 2013528064 | bytes 7340032 | tf_op jit(solution)/shard_map/dot_general | solution.py:70
  126.0 3.7 %collective-permute-done.11 = f32[512,768]{0,1:T(8,128)} collective-permute-done((f32[512,768]{0,1:T(8,128)}, f32[512,768]{0,1:T(8,128)}, u32[]{:S(2)}, u32[]{:S(2)}) %collective-permute-start.11) | collective-permute-done | bytes 1572896 | tf_op jit(solution)/shard_map/ppermute | solution.py:412
  129.7 2.9 %maximum_add_fusion = f32[512,768]{0,1:T(8,128)} fusion(f32[512,768]{0,1:T(8,128)} %collective-permute-done.11, f32[512,256]{0,1:T(8,128)S(1)} %get-tuple-element.250, f32[512,256]{0,1:T(8,128)S(1)} %get-tuple-element.248, f32[512,256]{0,1:T(8,128)S(1)} %get-tuple-element.246), kind=kLoop, calls=%fused_computation.14 | loop fusion | flops 1179648 | bytes 4718592 | tf_op jit(solution)/shard_map/add | solution.py:413
  132.6 1.9 copy.22
  136.5 1.7 collective-permute-start.14
  138.3 3.1 %add.320 = f32[4,160,1024]{2,1,0:T(8,128)S(1)} add(f32[4,160,1024]{2,1,0:T(8,128)} %get-tuple-element.193, f32[4,160,1024]{2,1,0:T(8,128)} %collective-permute-done.10) | non-fusion elementwise | flops 655360 | bytes 7864320 | tf_op jit(solution)/shard_map/add | solution.py:489
  141.5 6.7 %collective-permute-start.21 = (f32[80,1024]{1,0:T(8,128)S(1)}, f32[80,1024]{1,0:T(8,128)S(1)}, u32[]{:S(2)}, u32[]{:S(2)}) collective-permute-start(f32[80,1024]{1,0:T(8,128)S(1)} %get-tuple-element.240), channel_id=1, source_target_pairs={{0,2},{1,3},{2,4},{3,5},{4,6},{5,7},{6,0},{7,1},{8,10},{9,11},{10,... | collective-permute-start | bytes 983048 | tf_op jit(solution)/shard_map/ppermute | solution.py:62
  148.2 6.1 %collective-permute-start.23 = (f32[80,1024]{1,0:T(8,128)S(1)}, f32[80,1024]{1,0:T(8,128)S(1)}, u32[]{:S(2)}, u32[]{:S(2)}) collective-permute-start(f32[80,1024]{1,0:T(8,128)S(1)} %get-tuple-element.238), channel_id=1, source_target_pairs={{0,6},{1,7},{2,0},{3,1},{4,2},{5,3},{6,4},{7,5},{8,14},{9,15},{10,... | collective-permute-start | bytes 983048 | tf_op jit(solution)/shard_map/ppermute | solution.py:62
  156.5 5.1 %collective-permute-start.16 = (f32[4,8,768]{2,1,0:T(8,128)S(1)}, f32[4,8,768]{2,1,0:T(8,128)S(1)}, u32[]{:S(2)}, u32[]{:S(2)}) collective-permute-start(f32[4,8,768]{2,1,0:T(8,128)S(1)} %get-tuple-element.254), channel_id=1, source_target_pairs={{0,16},{1,65},{2,18},{3,67},{4,20},{5,69},{6,22},{7,71},{8,24},{9,... | collective-permute-start | bytes 294920 | tf_op jit(solution)/shard_map/ppermute | solution.py:62
  162.6 6.6 %collective-permute-start.24 = (f32[160,1024]{1,0:T(8,128)}, f32[160,1024]{1,0:T(8,128)S(1)}, u32[]{:S(2)}, u32[]{:S(2)}) collective-permute-start(f32[160,1024]{1,0:T(8,128)} %pad_maximum_fusion.4), channel_id=1, source_target_pairs={{0,6},{1,7},{2,0},{3,1},{4,2},{5,3},{6,4},{7,5},{8,14},{9,15},{10,... | collective-permute-start | bytes 1966088 | tf_op jit(solution)/shard_map/ppermute | solution.py:62
  170.2 3.8 %collective-permute-start.19 = (f32[8,768]{1,0:T(8,128)S(1)}, f32[8,768]{1,0:T(8,128)S(1)}, u32[]{:S(2)}, u32[]{:S(2)}) collective-permute-start(f32[8,768]{1,0:T(8,128)S(1)} %get-tuple-element.257), channel_id=1, source_target_pairs={{0,4},{1,5},{2,6},{3,7},{4,0},{5,1},{6,2},{7,3},{8,12},{9,13},{10,... | collective-permute-start | bytes 73736 | tf_op jit(solution)/shard_map/ppermute | solution.py:62
  174.2 12.7 %collective-permute-done.18 = f32[8,768]{1,0:T(8,128)S(1)} collective-permute-done((f32[8,768]{1,0:T(8,128)S(1)}, f32[8,768]{1,0:T(8,128)S(1)}, u32[]{:S(2)}, u32[]{:S(2)}) %collective-permute-start.18) | collective-permute-done | bytes 24608 | tf_op jit(solution)/shard_map/ppermute | solution.py:62
  188.8 2.8 %collective-permute-start.25 = (f32[4,768]{1,0:T(4,128)S(1)}, f32[4,768]{1,0:T(4,128)S(1)}, u32[]{:S(2)}, u32[]{:S(2)}) collective-permute-start(f32[4,768]{1,0:T(4,128)S(1)} %get-tuple-element.258), channel_id=1, source_target_pairs={{0,1},{1,0},{2,3},{3,2},{4,5},{5,4},{6,7},{7,6},{8,9},{9,8},{10,11... | collective-permute-start | bytes 36872 | tf_op jit(solution)/shard_map/ppermute | solution.py:428
  (100 shorter events, 27.2 us)
Async XLA Ops:
  0.8 14.4 %copy-start.10 = (s32[2,160]{1,0:T(2,128)S(1)}, s32[2,160]{1,0:T(2,128)}, u32[]{:S(2)}) copy-start(s32[2,160]{1,0:T(2,128)} %param.15) | copy-start | bytes 3844
  2.0 28.2 %collective-permute-start.8 = (f32[2,10,8,512]{3,2,1,0:T(8,128)S(1)}, f32[2,10,8,512]{3,2,1,0:T(8,128)S(1)}, u32[]{:S(2)}, u32[]{:S(2)}) collective-permute-start(f32[2,10,8,512]{3,2,1,0:T(8,128)S(1)} %get-tuple-element.236), channel_id=1, source_target_pairs={{0,0},{1,80},{2,8},{3,88},{4,16},{5,64},{6,24},{7,72},{8,48},{9,96... | collective-permute-start | bytes 983048 | tf_op jit(solution)/shard_map/ppermute | solution.py:449
  10.7 19.5 %collective-permute-start.9 = (f32[2,10,8,512]{3,2,1,0:T(8,128)S(1)}, f32[2,10,8,512]{3,2,1,0:T(8,128)}, u32[]{:S(2)}, u32[]{:S(2)}) collective-permute-start(f32[2,10,8,512]{3,2,1,0:T(8,128)S(1)} %get-tuple-element.235), channel_id=1, source_target_pairs={{0,40},{1,120},{2,48},{3,96},{4,56},{5,104},{6,32},{7,112},{8,8},{... | collective-permute-start | bytes 983048 | tf_op jit(solution)/shard_map/ppermute | solution.py:450
  16.8 13.4 %copy-start.3 = (f32[512,512]{1,0:T(8,128)S(1)}, f32[512,512]{1,0:T(8,128)}, u32[]{:S(2)}) copy-start(f32[512,512]{1,0:T(8,128)} %param.12) | copy-start | bytes 3145732
  32.8 8.5 %collective-permute-start.1 = (f32[32,8,512]{2,1,0:T(8,128)}, f32[32,8,512]{2,1,0:T(8,128)S(1)}, u32[]{:S(2)}, u32[]{:S(2)}) collective-permute-start(f32[32,8,512]{2,1,0:T(8,128)} %compact.3), channel_id=1, source_target_pairs={{0,24},{1,97},{2,26},{3,99},{4,28},{5,101},{6,30},{7,103},{8,0},{9... | collective-permute-start | bytes 1572872 | tf_op jit(solution)/shard_map/while/body/ppermute | solution.py:62
  34.5 9.8 %collective-permute-start = (f32[32,8,512]{2,1,0:T(8,128)}, f32[32,8,512]{2,1,0:T(8,128)S(1)}, u32[]{:S(2)}, u32[]{:S(2)}) collective-permute-start(f32[32,8,512]{2,1,0:T(8,128)} %compact.3), channel_id=1, source_target_pairs={{0,8},{1,33},{2,10},{3,35},{4,12},{5,37},{6,14},{7,39},{8,16},{9,4... | collective-permute-start | bytes 1572872 | tf_op jit(solution)/shard_map/while/body/ppermute | solution.py:62
  41.4 6.3 %collective-permute-start.2 = (f32[16,8,512]{2,1,0:T(8,128)S(1)}, f32[16,8,512]{2,1,0:T(8,128)S(1)}, u32[]{:S(2)}, u32[]{:S(2)}) collective-permute-start(f32[16,8,512]{2,1,0:T(8,128)S(1)} %slice.116), channel_id=1, source_target_pairs={{0,24},{1,97},{2,26},{3,99},{4,28},{5,101},{6,30},{7,103},{8,0},{9... | collective-permute-start | bytes 786440 | tf_op jit(solution)/shard_map/while/body/ppermute | solution.py:62
  44.4 10.6 %copy-start.4 = (f32[512,512]{1,0:T(8,128)S(1)}, f32[512,512]{1,0:T(8,128)}, u32[]{:S(2)}) copy-start(f32[512,512]{1,0:T(8,128)} %get-tuple-element.358) | copy-start | bytes 3145732 | tf_op jit(solution)/shard_map/while
  44.4 6.5 %collective-permute-start.3 = (f32[16,8,512]{2,1,0:T(8,128)S(1)}, f32[16,8,512]{2,1,0:T(8,128)S(1)}, u32[]{:S(2)}, u32[]{:S(2)}) collective-permute-start(f32[16,8,512]{2,1,0:T(8,128)S(1)} %slice.117), channel_id=1, source_target_pairs={{0,8},{1,33},{2,10},{3,35},{4,12},{5,37},{6,14},{7,39},{8,16},{9,4... | collective-permute-start | bytes 786440 | tf_op jit(solution)/shard_map/while/body/ppermute | solution.py:62
  52.2 27.6 %copy-start = (f32[4,32,8,512]{3,2,1,0:T(8,128)}, f32[4,32,8,512]{3,2,1,0:T(8,128)S(1)}, u32[]{:S(2)}) copy-start(f32[4,32,8,512]{3,2,1,0:T(8,128)S(1)} %pad_maximum_fusion.7.own) | copy-start | bytes 6291460 | tf_op jit(solution)/shard_map/while
  52.2 26.5 %collective-permute-start.4 = (f32[4,32,8,512]{3,2,1,0:T(8,128)S(1)}, f32[4,32,8,512]{3,2,1,0:T(8,128)S(1)}, u32[]{:S(2)}, u32[]{:S(2)}) collective-permute-start(f32[4,32,8,512]{3,2,1,0:T(8,128)S(1)} %pad_maximum_fusion.7.own), channel_id=1, source_target_pairs={{0,32},{1,9},{2,34},{3,11},{4,36},{5,13},{6,38},{7,15},{8,40},{9,1... | collective-permute-start | bytes 6291464 | tf_op jit(solution)/shard_map/while/body/ppermute | solution.py:62
  53.2 25.4 %collective-permute-start.5 = (f32[4,32,8,512]{3,2,1,0:T(8,128)S(1)}, f32[4,32,8,512]{3,2,1,0:T(8,128)S(1)}, u32[]{:S(2)}, u32[]{:S(2)}) collective-permute-start(f32[4,32,8,512]{3,2,1,0:T(8,128)S(1)} %pad_maximum_fusion.7.own), channel_id=1, source_target_pairs={{0,96},{1,25},{2,98},{3,27},{4,100},{5,29},{6,102},{7,31},{8,104},... | collective-permute-start | bytes 6291464 | tf_op jit(solution)/shard_map/while/body/ppermute | solution.py:62
  78.6 17.3 %copy-start.1 = (f32[4,32,8,512]{3,2,1,0:T(8,128)}, f32[4,32,8,512]{3,2,1,0:T(8,128)S(1)}, u32[]{:S(2)}) copy-start(f32[4,32,8,512]{3,2,1,0:T(8,128)S(1)} %collective-permute-done.4.before) | copy-start | bytes 6291460 | tf_op jit(solution)/shard_map/while
  79.7 15.5 %collective-permute-start.6 = (f32[2,32,8,512]{3,2,1,0:T(8,128)}, f32[2,32,8,512]{3,2,1,0:T(8,128)}, u32[]{:S(2)}, u32[]{:S(2)}) collective-permute-start(f32[2,32,8,512]{3,2,1,0:T(8,128)} %slice.118), channel_id=1, source_target_pairs={{0,32},{1,9},{2,34},{3,11},{4,36},{5,13},{6,38},{7,15},{8,40},{9,1... | collective-permute-start | bytes 3145736 | tf_op jit(solution)/shard_map/while/body/ppermute | solution.py:62
  81.5 14.4 %collective-permute-start.7 = (f32[2,32,8,512]{3,2,1,0:T(8,128)}, f32[2,32,8,512]{3,2,1,0:T(8,128)}, u32[]{:S(2)}, u32[]{:S(2)}) collective-permute-start(f32[2,32,8,512]{3,2,1,0:T(8,128)} %slice.119), channel_id=1, source_target_pairs={{0,96},{1,25},{2,98},{3,27},{4,100},{5,29},{6,102},{7,31},{8,104},... | collective-permute-start | bytes 3145736 | tf_op jit(solution)/shard_map/while/body/ppermute | solution.py:62
  106.6 31.6 %collective-permute-start.10 = (f32[4,160,1024]{2,1,0:T(8,128)}, f32[4,160,1024]{2,1,0:T(8,128)}, u32[]{:S(2)}, u32[]{:S(2)}) collective-permute-start(f32[4,160,1024]{2,1,0:T(8,128)} %get-tuple-element.194), channel_id=1, source_target_pairs={{0,1},{1,0},{2,3},{3,2},{4,5},{5,4},{6,7},{7,6},{8,9},{9,8},{10,11... | collective-permute-start | bytes 7864328 | tf_op jit(solution)/shard_map/ppermute | solution.py:489
  126.0 3.8 %collective-permute-start.11 = (f32[512,768]{0,1:T(8,128)}, f32[512,768]{0,1:T(8,128)}, u32[]{:S(2)}, u32[]{:S(2)}) collective-permute-start(f32[512,768]{0,1:T(8,128)} %pad_maximum_fusion.2), channel_id=1, source_target_pairs={{0,1},{1,0},{2,3},{3,2},{4,5},{5,4},{6,7},{7,6},{8,9},{9,8},{10,11... | collective-permute-start | bytes 4718600 | tf_op jit(solution)/shard_map/ppermute | solution.py:412
  135.6 18.7 %collective-permute-start.12 = (f32[4,4,8,768]{3,2,1,0:T(8,128)}, f32[4,4,8,768]{3,2,1,0:T(8,128)S(1)}, u32[]{:S(2)}, u32[]{:S(2)}) collective-permute-start(f32[4,4,8,768]{3,2,1,0:T(8,128)} %get-tuple-element.243), channel_id=1, source_target_pairs={{0,32},{1,9},{2,34},{3,11},{4,36},{5,13},{6,38},{7,15},{8,40},{9,1... | collective-permute-start | bytes 1179656 | tf_op jit(solution)/shard_map/ppermute | solution.py:62
  135.6 18.7 %collective-permute-start.13 = (f32[4,4,8,768]{3,2,1,0:T(8,128)}, f32[4,4,8,768]{3,2,1,0:T(8,128)S(1)}, u32[]{:S(2)}, u32[]{:S(2)}) collective-permute-start(f32[4,4,8,768]{3,2,1,0:T(8,128)} %get-tuple-element.244), channel_id=1, source_target_pairs={{0,64},{1,17},{2,66},{3,19},{4,68},{5,21},{6,70},{7,23},{8,72},{9,... | collective-permute-start | bytes 1179656 | tf_op jit(solution)/shard_map/ppermute | solution.py:62
  136.5 18.5 %collective-permute-start.14 = (f32[4,4,8,768]{3,2,1,0:T(8,128)}, f32[4,4,8,768]{3,2,1,0:T(8,128)}, u32[]{:S(2)}, u32[]{:S(2)}) collective-permute-start(f32[4,4,8,768]{3,2,1,0:T(8,128)} %get-tuple-element.245), channel_id=1, source_target_pairs={{0,96},{1,25},{2,98},{3,27},{4,100},{5,29},{6,102},{7,31},{8,104},... | collective-permute-start | bytes 1179656 | tf_op jit(solution)/shard_map/ppermute | solution.py:62
  141.4 20.2 %copy-start.7 = (f32[4,160,1024]{2,1,0:T(8,128)}, f32[4,160,1024]{2,1,0:T(8,128)S(1)}, u32[]{:S(2)}) copy-start(f32[4,160,1024]{2,1,0:T(8,128)S(1)} %add.320) | copy-start | bytes 7864324
  141.5 20.1 %collective-permute-start.21 = (f32[80,1024]{1,0:T(8,128)S(1)}, f32[80,1024]{1,0:T(8,128)S(1)}, u32[]{:S(2)}, u32[]{:S(2)}) collective-permute-start(f32[80,1024]{1,0:T(8,128)S(1)} %get-tuple-element.240), channel_id=1, source_target_pairs={{0,2},{1,3},{2,4},{3,5},{4,6},{5,7},{6,0},{7,1},{8,10},{9,11},{10,... | collective-permute-start | bytes 983048 | tf_op jit(solution)/shard_map/ppermute | solution.py:62
  148.2 13.4 %collective-permute-start.23 = (f32[80,1024]{1,0:T(8,128)S(1)}, f32[80,1024]{1,0:T(8,128)S(1)}, u32[]{:S(2)}, u32[]{:S(2)}) collective-permute-start(f32[80,1024]{1,0:T(8,128)S(1)} %get-tuple-element.238), channel_id=1, source_target_pairs={{0,6},{1,7},{2,0},{3,1},{4,2},{5,3},{6,4},{7,5},{8,14},{9,15},{10,... | collective-permute-start | bytes 983048 | tf_op jit(solution)/shard_map/ppermute | solution.py:62
  156.3 13.8 %collective-permute-start.15 = (f32[4,8,768]{2,1,0:T(8,128)S(1)}, f32[4,8,768]{2,1,0:T(8,128)S(1)}, u32[]{:S(2)}, u32[]{:S(2)}) collective-permute-start(f32[4,8,768]{2,1,0:T(8,128)S(1)} %get-tuple-element.252), channel_id=1, source_target_pairs={{0,8},{1,33},{2,10},{3,35},{4,12},{5,37},{6,14},{7,39},{8,16},{9,4... | collective-permute-start | bytes 294920 | tf_op jit(solution)/shard_map/ppermute | solution.py:62
  156.5 13.6 %collective-permute-start.16 = (f32[4,8,768]{2,1,0:T(8,128)S(1)}, f32[4,8,768]{2,1,0:T(8,128)S(1)}, u32[]{:S(2)}, u32[]{:S(2)}) collective-permute-start(f32[4,8,768]{2,1,0:T(8,128)S(1)} %get-tuple-element.254), channel_id=1, source_target_pairs={{0,16},{1,65},{2,18},{3,67},{4,20},{5,69},{6,22},{7,71},{8,24},{9,... | collective-permute-start | bytes 294920 | tf_op jit(solution)/shard_map/ppermute | solution.py:62
  161.6 8.5 %collective-permute-start.17 = (f32[4,8,768]{2,1,0:T(8,128)S(1)}, f32[4,8,768]{2,1,0:T(8,128)S(1)}, u32[]{:S(2)}, u32[]{:S(2)}) collective-permute-start(f32[4,8,768]{2,1,0:T(8,128)S(1)} %get-tuple-element.253), channel_id=1, source_target_pairs={{0,24},{1,97},{2,26},{3,99},{4,28},{5,101},{6,30},{7,103},{8,0},{9... | collective-permute-start | bytes 294920 | tf_op jit(solution)/shard_map/ppermute | solution.py:62
  162.6 24.3 %collective-permute-start.24 = (f32[160,1024]{1,0:T(8,128)}, f32[160,1024]{1,0:T(8,128)S(1)}, u32[]{:S(2)}, u32[]{:S(2)}) collective-permute-start(f32[160,1024]{1,0:T(8,128)} %pad_maximum_fusion.4), channel_id=1, source_target_pairs={{0,6},{1,7},{2,0},{3,1},{4,2},{5,3},{6,4},{7,5},{8,14},{9,15},{10,... | collective-permute-start | bytes 1966088 | tf_op jit(solution)/shard_map/ppermute | solution.py:62
  170.1 16.8 %collective-permute-start.22 = (f32[160,1024]{1,0:T(8,128)}, f32[160,1024]{1,0:T(8,128)S(1)}, u32[]{:S(2)}, u32[]{:S(2)}) collective-permute-start(f32[160,1024]{1,0:T(8,128)} %pad_maximum_fusion.3), channel_id=1, source_target_pairs={{0,2},{1,3},{2,4},{3,5},{4,6},{5,7},{6,0},{7,1},{8,10},{9,11},{10,... | collective-permute-start | bytes 1966088 | tf_op jit(solution)/shard_map/ppermute | solution.py:62
  170.1 16.7 %collective-permute-start.18 = (f32[8,768]{1,0:T(8,128)S(1)}, f32[8,768]{1,0:T(8,128)S(1)}, u32[]{:S(2)}, u32[]{:S(2)}) collective-permute-start(f32[8,768]{1,0:T(8,128)S(1)} %get-tuple-element.255), channel_id=1, source_target_pairs={{0,2},{1,3},{2,4},{3,5},{4,6},{5,7},{6,0},{7,1},{8,10},{9,11},{10,... | collective-permute-start | bytes 73736 | tf_op jit(solution)/shard_map/ppermute | solution.py:62
  170.2 16.6 %collective-permute-start.19 = (f32[8,768]{1,0:T(8,128)S(1)}, f32[8,768]{1,0:T(8,128)S(1)}, u32[]{:S(2)}, u32[]{:S(2)}) collective-permute-start(f32[8,768]{1,0:T(8,128)S(1)} %get-tuple-element.257), channel_id=1, source_target_pairs={{0,4},{1,5},{2,6},{3,7},{4,0},{5,1},{6,2},{7,3},{8,12},{9,13},{10,... | collective-permute-start | bytes 73736 | tf_op jit(solution)/shard_map/ppermute | solution.py:62
  174.1 12.8 %collective-permute-start.20 = (f32[8,768]{1,0:T(8,128)S(1)}, f32[8,768]{1,0:T(8,128)S(1)}, u32[]{:S(2)}, u32[]{:S(2)}) collective-permute-start(f32[8,768]{1,0:T(8,128)S(1)} %get-tuple-element.256), channel_id=1, source_target_pairs={{0,6},{1,7},{2,0},{3,1},{4,2},{5,3},{6,4},{7,5},{8,14},{9,15},{10,... | collective-permute-start | bytes 73736 | tf_op jit(solution)/shard_map/ppermute | solution.py:62
  188.8 4.0 %collective-permute-start.25 = (f32[4,768]{1,0:T(4,128)S(1)}, f32[4,768]{1,0:T(4,128)S(1)}, u32[]{:S(2)}, u32[]{:S(2)}) collective-permute-start(f32[4,768]{1,0:T(4,128)S(1)} %get-tuple-element.258), channel_id=1, source_target_pairs={{0,1},{1,0},{2,3},{3,2},{4,5},{5,4},{6,7},{7,6},{8,9},{9,8},{10,11... | collective-permute-start | bytes 36872 | tf_op jit(solution)/shard_map/ppermute | solution.py:428
  (7 other events, 22.0 us)
